TPU v7x, 32 devices: a whole 2x2x4 slice. The times are simulated.
32 devices in a mesh: crop: 1, res: 32 (over z, y, x, core).
Axes of the slice: x: 2, y: 2, z: 4, core: 2. Of those that a mesh axis runs over, the one named last changes fastest.
Arguments:
- homolog_symbol_ids: int32 [64, 128], P(('crop', 'res')), may hold values from 0 to 22
- residue_attend_mask: int32 [128], P('crop'), may hold values 0 or 1
- alignment_state: bfloat16 [64, 128, 256], P(('crop', 'res')), may hold values from -6 to 6
- pair: bfloat16 [128, 128, 128], P(('crop', 'res')), may hold values from -6 to 6
- symbol_lookup_matrix: bfloat16 [23, 256], replicated, may hold values from -3 to 3
- pair_bias_weight: bfloat16 [128, 8], replicated, may hold values from -0.5 to 0.5
- row_projection_weight: bfloat16 [256, 1024], replicated, may hold values from -8 to 8
- horizontal_readout_matrix: bfloat16 [256, 256], replicated, may hold values from -0.375 to 0.375
- column_projection_weight: bfloat16 [256, 1024], replicated, may hold values from -8 to 8
- vertical_readout_matrix: bfloat16 [256, 256], replicated, may hold values from -0.375 to 0.375
- product_factor_matrices: bfloat16 [256, 64], replicated, may hold values from -0.375 to 0.375
- outer_output_weight: bfloat16 [1024, 128], replicated, may hold values from -1.5 to 1.5
- triangle_input_weight: bfloat16 [128, 640], replicated, may hold values from -0.5 to 0.5
- triangle_output_weight: bfloat16 [128, 128], replicated, may hold values from -0.5 to 0.5
Outputs:
- alignment_output: bfloat16 [64, 128, 256], P('crop', 'res')
- pair_output: bfloat16 [128, 128, 128], P(('crop', 'res'))
All inputs are finite; a program needn't handle non-finite values.
Results may differ from a plain program's by a relative error of at most 0.013.
Values may be sent and summed in bfloat16 or wider, within the bound.
A program may use at most 64 MiB of HBM per device.

v0:
```python
import jax
import jax.numpy as jnp
from jax import lax
from jax.sharding import PartitionSpec as P

EPSILON = 1e-05


def layer_normalized(input_rows, axis):
    average = jnp.mean(input_rows, axis, keepdims=True)
    centred = input_rows - average
    spread = jnp.mean(centred * centred, axis, keepdims=True)
    return centred * lax.rsqrt(spread + EPSILON)


def split_proj(input_rows, weight, head_count):
    channels = weight.shape[0]
    head_size = channels // head_count
    projected = jnp.einsum("blc,ce->ble", input_rows, weight, preferred_element_type=jnp.float32)
    lead = projected.shape[:2]
    query_tensor = (
        (projected[..., :channels] * head_size ** (-0.5))
        .astype(jnp.bfloat16)
        .reshape(lead + (head_count, head_size))
    )
    key_tensor = (
        projected[..., channels : 2 * channels]
        .astype(jnp.bfloat16)
        .reshape(lead + (head_count, head_size))
    )
    value_tensor = (
        projected[..., 2 * channels : 3 * channels]
        .astype(jnp.bfloat16)
        .reshape(lead + (head_count, head_size))
    )
    gate_values = projected[..., 3 * channels :]
    return (query_tensor, key_tensor, value_tensor, gate_values)


def attention_block_fn(query_tensor, key_tensor, value_tensor, gate_values, extra_bias, out_weight):
    scores = (
        jnp.einsum("bqhd,bkhd->bhqk", query_tensor, key_tensor, preferred_element_type=jnp.float32)
        + extra_bias
    )
    row_top = jnp.max(scores, -1, keepdims=True)
    exp_scores = jnp.exp(scores - row_top)
    weights = (exp_scores / jnp.sum(exp_scores, -1, keepdims=True)).astype(jnp.bfloat16)
    mixed = jnp.einsum("bhqk,bkhd->bqhd", weights, value_tensor, preferred_element_type=jnp.float32)
    gated = (jax.nn.sigmoid(gate_values) * mixed.reshape(gate_values.shape)).astype(jnp.bfloat16)
    return jnp.einsum("bqc,ce->bqe", gated, out_weight, preferred_element_type=jnp.float32)


def shards(
    homolog_symbol_ids,
    residue_attend_mask,
    alignment_state,
    pair,
    symbol_lookup_matrix,
    pair_bias_weight,
    row_projection_weight,
    horizontal_readout_matrix,
    column_projection_weight,
    vertical_readout_matrix,
    product_factor_matrices,
    outer_output_weight,
    triangle_input_weight,
    triangle_output_weight,
):
    residue_count = lax.axis_size("res")
    sequence_total = alignment_state.shape[0] * residue_count
    res_local = pair.shape[0]
    chain_total = pair.shape[1]
    pair_chan = pair.shape[2]
    owner_chan = pair_chan // residue_count
    outer_chan = product_factor_matrices.shape[1] // 2
    head_count = pair_bias_weight.shape[1]
    token_class_count = symbol_lookup_matrix.shape[0]
    one_hot_tokens = (
        homolog_symbol_ids[:, :, None]
        == jnp.arange(token_class_count, dtype=jnp.int32)[None, None, :]
    ).astype(jnp.bfloat16)
    alignment_initial = alignment_state.astype(jnp.float32) + jnp.einsum(
        "kly,yb->klb", one_hot_tokens, symbol_lookup_matrix, preferred_element_type=jnp.float32
    )
    pair_normed = layer_normalized(pair.astype(jnp.float32), -1).astype(jnp.bfloat16)
    bias_local = jnp.einsum(
        "ijc,ch->hij", pair_normed, pair_bias_weight, preferred_element_type=jnp.float32
    ).astype(jnp.bfloat16)
    mask_bias = (residue_attend_mask.astype(jnp.float32) - 1.0) * 10000.0
    row_input = layer_normalized(alignment_initial, -1).astype(jnp.bfloat16)
    query_tensor, key_tensor, value_tensor, gate_values = split_proj(
        row_input, row_projection_weight, head_count
    )
    bias_all = lax.all_gather(bias_local, "res", axis=1, tiled=True)
    extra_bias = bias_all.astype(jnp.float32)[None] + mask_bias[None, None, None, :]
    row_attention_update = attention_block_fn(
        query_tensor, key_tensor, value_tensor, gate_values, extra_bias, horizontal_readout_matrix
    )
    alignment_after_rows = (alignment_initial + row_attention_update).astype(jnp.bfloat16)
    alignment_columns = lax.all_to_all(
        alignment_after_rows, "res", split_axis=1, concat_axis=0, tiled=True
    )
    column_start = jnp.swapaxes(alignment_columns, 0, 1).astype(jnp.float32)
    col_in = layer_normalized(column_start, -1).astype(jnp.bfloat16)
    col_queries, col_keys, col_values, col_gating = split_proj(
        col_in, column_projection_weight, head_count
    )
    alignment_after_columns = column_start + attention_block_fn(
        col_queries, col_keys, col_values, col_gating, jnp.float32(0.0), vertical_readout_matrix
    )
    alignment_output = jnp.swapaxes(alignment_after_columns, 0, 1).astype(jnp.bfloat16)
    outer_input = layer_normalized(alignment_after_columns, -1).astype(jnp.bfloat16)
    factor_ab = jnp.einsum(
        "rsc,ce->rse", outer_input, product_factor_matrices, preferred_element_type=jnp.float32
    )
    left = factor_ab[..., :outer_chan].astype(jnp.bfloat16)
    latter_factor = (
        factor_ab[..., outer_chan:]
        .astype(jnp.bfloat16)
        .reshape(res_local, sequence_total * outer_chan)
    )
    piece = lax.all_gather(latter_factor, "res", axis=0, tiled=True)
    count = piece.shape[0]
    right_rows = piece.reshape(count, sequence_total, outer_chan)
    cross_product_result = (
        jnp.einsum("isc,jsd->ijcd", left, right_rows, preferred_element_type=jnp.float32)
        / sequence_total
    ).astype(jnp.bfloat16)
    update = jnp.einsum(
        "ije,ez->ijz",
        cross_product_result.reshape(res_local, count, outer_chan * outer_chan),
        outer_output_weight,
        preferred_element_type=jnp.float32,
    )
    pair_one = pair.astype(jnp.float32) + update
    tri_normed = layer_normalized(pair_one, -1).astype(jnp.bfloat16)
    factors = jnp.einsum(
        "ijc,ce->eij",
        tri_normed,
        triangle_input_weight[:, : 4 * pair_chan],
        preferred_element_type=jnp.float32,
    )
    gate_out = jnp.einsum(
        "ijc,ce->ije",
        tri_normed,
        triangle_input_weight[:, 4 * pair_chan :],
        preferred_element_type=jnp.float32,
    )
    left_f = (jax.nn.sigmoid(factors[pair_chan : 2 * pair_chan]) * factors[:pair_chan]).astype(
        jnp.bfloat16
    )
    right_f = (
        jax.nn.sigmoid(factors[3 * pair_chan :]) * factors[2 * pair_chan : 3 * pair_chan]
    ).astype(jnp.bfloat16)
    left_f = left_f.reshape(residue_count, owner_chan, res_local, chain_total)
    right_f = right_f.reshape(residue_count, owner_chan, res_local, chain_total)
    combined = jnp.einsum(
        "xcik,xcjk->xcij",
        lax.all_to_all(left_f, "res", split_axis=0, concat_axis=2, tiled=True),
        lax.all_to_all(right_f, "res", split_axis=0, concat_axis=2, tiled=True),
        preferred_element_type=jnp.float32,
    ).astype(jnp.bfloat16)
    back_rows = lax.all_to_all(combined, "res", split_axis=2, concat_axis=0, tiled=True)
    back_rows = back_rows.reshape(pair_chan, res_local, chain_total)
    comb_normed = layer_normalized(back_rows.astype(jnp.float32), 0).astype(jnp.bfloat16)
    tri_update = jnp.einsum(
        "cij,cz->ijz", comb_normed, triangle_output_weight, preferred_element_type=jnp.float32
    )
    pair_output = (pair_one + jax.nn.sigmoid(gate_out) * tri_update).astype(jnp.bfloat16)
    return (alignment_output, pair_output)


def solution(mesh):
    placed = (
        P(("crop", "res"), None),
        P("crop"),
        P(("crop", "res"), None, None),
        P(("crop", "res"), None, None),
        P(),
        P(),
        P(),
        P(),
        P(),
        P(),
        P(),
        P(),
        P(),
        P(),
    )
    return jax.shard_map(
        shards,
        mesh=mesh,
        in_specs=placed,
        out_specs=(P("crop", "res", None), P(("crop", "res"), None, None)),
        check_vma=False,
    )
```

profile of v0, /device:TPU:0, one launch (start us, length us, event | category | flops | bytes accessed | tf_op | source)
XLA Modules:
  0.0 155.3 jit_solution(11216174859262117624)
XLA Ops:
  0.7 0.7 add_multiply_fusion
  1.4 1.0 copy.74
  2.5 0.8 fusion.14
  3.4 43.9 %all_gather.6 = bf16[8,128,128]{2,0,1:T(8,128)(2,1)S(1)} all-gather(bf16[8,4,128]{2,0,1:T(8,128)(2,1)S(1)} %fusion.14), channel_id=1, replica_groups=mesh['crop'=1,'res'=32] {'res'}, dimensions={1}, use_global_device_ids=true | all-gather | bytes 270336 | tf_op jit(solution)/shard_map/all_gather | solution.py:94
  47.3 0.2 copy.76
  47.6 0.3 fusion.84
  47.9 0.2 multiply_reduce_fusion.3
  48.1 0.3 fusion.85
  48.5 0.7 fusion.83
  49.2 0.1 copy.73
  49.3 0.1 copy.72
  49.5 0.5 copy-done.1
  49.9 0.2 copy-done.2
  50.1 0.5 fusion.86
  50.6 1.3 convolution_add_fusion
  51.9 1.0 copy.71
  53.0 1.0 fusion.20
  54.0 1.1 copy.78
  55.2 1.1 fusion.11
  56.3 0.1 copy.79
  56.4 9.9 %all_to_all.48 = bf16[2,128,256]{2,0,1:T(2,128)(2,1)S(1)} all-to-all(bf16[2,128,256]{2,0,1:T(2,128)(2,1)S(1)} %copy.79), channel_id=1, replica_groups=mesh['crop'=1,'res'=32] {'res'}, dimensions={1} | all-to-all | bytes 262144 | tf_op jit(solution)/shard_map/all_to_all | solution.py:100
  66.4 0.2 reshape.167
  66.6 0.1 bitcast_reduce_fusion.1
  66.7 0.2 multiply_reduce_fusion.2
  66.9 0.3 fusion.87
  67.3 0.7 fusion.82
  68.0 0.2 copy.83
  68.2 0.2 copy.82
  68.4 0.5 fusion.88
  68.9 0.3 fusion.90
  69.2 1.1 copy.81
  70.3 1.2 fusion.19
  71.4 1.2 copy.85
  72.7 1.1 fusion.46
  73.8 0.1 fusion.81
  73.9 0.2 multiply_reduce_fusion.1
  74.1 0.3 convolution_convert_fusion.1
  74.4 0.1 copy.86
  74.5 0.1 reshape.173
  74.7 39.3 %all-gather = bf16[32,4,2048]{2,1,0:T(4,128)(2,1)S(1)} all-gather(bf16[1,4,2048]{2,1,0:T(4,128)(2,1)S(1)} %reshape.173), channel_id=1, replica_groups=mesh['crop'=1,'res'=32] {'res'}, dimensions={0}, use_global_device_ids=true | all-gather | bytes 540672 | tf_op jit(solution)/shard_map/all_gather | solution.py:122
  114.0 1.2 reshape.160
  115.2 2.6 %copy.109 = bf16[128,64,32,1]{0,1,3,2:T(8,128)(2,1)S(1)} copy(bf16[128,64,32,1]{2,1,0,3:T(8,128)(2,1)S(1)} %bitcast.133) | data formatting | bytes 1048576 | tf_op jit(solution)/shard_map/reshape | solution.py:124
  117.8 0.4 fusion.6
  118.2 0.7 copy.88
  118.9 0.4 fusion.89
  119.4 0.3 convolution_bitcast_fusion
  119.7 0.1 fusion.25
  119.8 0.1 copy.97
  120.0 0.7 copy.98
  120.7 2.6 %all-to-all-start.2 = ((bf16[32,4,4,128]{3,1,2,0:T(4,128)(2,1)}), bf16[32,4,4,128]{3,1,2,0:T(4,128)(2,1)S(1)}, u32[]{:S(2)}, u32[]{:S(2)}) async-start(bf16[32,4,4,128]{3,1,2,0:T(4,128)(2,1)} %copy.98), calls=%async_computation.2 | async-start | bytes 262144 | tf_op jit(solution)/shard_map/all_to_all | solution.py:160
  123.3 0.1 copy.94
  123.4 0.7 copy.95
  124.1 7.4 %all-to-all-done.2 = bf16[32,4,4,128]{3,1,2,0:T(4,128)(2,1)S(1)} async-done(((bf16[32,4,4,128]{3,1,2,0:T(4,128)(2,1)}), bf16[32,4,4,128]{3,1,2,0:T(4,128)(2,1)S(1)}, u32[]{:S(2)}, u32[]{:S(2)}) %all-to-all-start.2) | async-done | bytes 131104 | tf_op jit(solution)/shard_map/all_to_all | solution.py:160
  131.5 2.6 %all-to-all-start.1 = ((bf16[32,4,4,128]{3,1,2,0:T(4,128)(2,1)}), bf16[32,4,4,128]{3,1,2,0:T(4,128)(2,1)S(1)}, u32[]{:S(2)}, u32[]{:S(2)}) async-start(bf16[32,4,4,128]{3,1,2,0:T(4,128)(2,1)} %copy.95), calls=%async_computation.1 | async-start | bytes 262144 | tf_op jit(solution)/shard_map/all_to_all | solution.py:159
  134.1 8.1 %all-to-all-done.1 = bf16[32,4,4,128]{3,1,2,0:T(4,128)(2,1)S(1)} async-done(((bf16[32,4,4,128]{3,1,2,0:T(4,128)(2,1)}), bf16[32,4,4,128]{3,1,2,0:T(4,128)(2,1)S(1)}, u32[]{:S(2)}, u32[]{:S(2)}) %all-to-all-start.1) | async-done | bytes 131104 | tf_op jit(solution)/shard_map/all_to_all | solution.py:159
  142.3 0.2 fusion.13
  142.5 0.8 copy.100
  143.3 2.6 %all-to-all-start.3 = ((bf16[1,4,128,128]{3,1,0,2:T(4,128)(2,1)}), bf16[1,4,128,128]{3,1,0,2:T(4,128)(2,1)S(1)}, u32[]{:S(2)}, u32[]{:S(2)}) async-start(bf16[1,4,128,128]{3,1,0,2:T(4,128)(2,1)} %copy.100), calls=%async_computation.3 | async-start | bytes 262144 | tf_op jit(solution)/shard_map/all_to_all | solution.py:163
  145.9 0.8 copy.104
  146.6 0.3 fusion.10
  146.9 7.2 %all-to-all-done.3 = bf16[1,4,128,128]{3,1,0,2:T(4,128)(2,1)S(1)} async-done(((bf16[1,4,128,128]{3,1,0,2:T(4,128)(2,1)}), bf16[1,4,128,128]{3,1,0,2:T(4,128)(2,1)S(1)}, u32[]{:S(2)}, u32[]{:S(2)}) %all-to-all-start.3) | async-done | bytes 131104 | tf_op jit(solution)/shard_map/all_to_all | solution.py:163
  154.2 0.1 fusion.44
  154.3 0.2 fusion.12
  154.6 0.8 copy.105
  (44 shorter events, 0.6 us)
Async XLA Ops:
  0.6 47.5 %copy-start = (bf16[256,1024]{1,0:T(8,128)(2,1)S(1)}, bf16[256,1024]{1,0:T(8,128)(2,1)}, u32[]{:S(2)}) copy-start(bf16[256,1024]{1,0:T(8,128)(2,1)} %param.20) | copy-start | bytes 1572868
  0.6 46.9 %copy-start.9 = (bf16[23,256]{1,0:T(8,128)(2,1)S(1)}, bf16[23,256]{1,0:T(8,128)(2,1)}, u32[]{:S(2)}) copy-start(bf16[23,256]{1,0:T(8,128)(2,1)} %param.18) | copy-start | bytes 35332
  0.7 46.9 %copy-start.5 = (bf16[2,128,256]{2,1,0:T(8,128)(2,1)S(1)}, bf16[2,128,256]{2,1,0:T(8,128)(2,1)}, u32[]{:S(2)}) copy-start(bf16[2,128,256]{2,1,0:T(8,128)(2,1)} %param.16) | copy-start | bytes 393220
  0.7 46.9 %copy-start.10 = (s32[2,128]{1,0:T(2,128)S(1)}, s32[2,128]{1,0:T(2,128)}, u32[]{:S(2)}) copy-start(s32[2,128]{1,0:T(2,128)} %param.14) | copy-start | bytes 3076
  49.3 0.6 copy-start.1
  49.5 0.7 copy-start.2
  54.0 12.9 %copy-start.3 = (bf16[256,1024]{1,0:T(8,128)(2,1)S(1)}, bf16[256,1024]{1,0:T(8,128)(2,1)}, u32[]{:S(2)}) copy-start(bf16[256,1024]{1,0:T(8,128)(2,1)} %param.22) | copy-start | bytes 1572868
  71.4 2.7 %copy-start.7 = (bf16[256,64]{0,1:T(8,128)(2,1)S(1)}, bf16[256,64]{0,1:T(8,128)(2,1)}, u32[]{:S(2)}) copy-start(bf16[256,64]{0,1:T(8,128)(2,1)} %param.24) | copy-start | bytes 98308
  117.8 1.1 copy-start.4
  118.2 1.1 copy-start.6
  120.7 10.8 %all-to-all-start.2 = ((bf16[32,4,4,128]{3,1,2,0:T(4,128)(2,1)}), bf16[32,4,4,128]{3,1,2,0:T(4,128)(2,1)S(1)}, u32[]{:S(2)}, u32[]{:S(2)}) async-start(bf16[32,4,4,128]{3,1,2,0:T(4,128)(2,1)} %copy.98), calls=%async_computation.2 | async-start | bytes 262144 | tf_op jit(solution)/shard_map/all_to_all | solution.py:160
  123.4 30.9 %copy-start.8 = (bf16[128,128]{1,0:T(8,128)(2,1)S(1)}, bf16[128,128]{1,0:T(8,128)(2,1)}, u32[]{:S(2)}) copy-start(bf16[128,128]{1,0:T(8,128)(2,1)} %param.27) | copy-start | bytes 98308
  131.5 10.8 %all-to-all-start.1 = ((bf16[32,4,4,128]{3,1,2,0:T(4,128)(2,1)}), bf16[32,4,4,128]{3,1,2,0:T(4,128)(2,1)S(1)}, u32[]{:S(2)}, u32[]{:S(2)}) async-start(bf16[32,4,4,128]{3,1,2,0:T(4,128)(2,1)} %copy.95), calls=%async_computation.1 | async-start | bytes 262144 | tf_op jit(solution)/shard_map/all_to_all | solution.py:159
  143.3 10.8 %all-to-all-start.3 = ((bf16[1,4,128,128]{3,1,0,2:T(4,128)(2,1)}), bf16[1,4,128,128]{3,1,0,2:T(4,128)(2,1)S(1)}, u32[]{:S(2)}, u32[]{:S(2)}) async-start(bf16[1,4,128,128]{3,1,0,2:T(4,128)(2,1)} %copy.100), calls=%async_computation.3 | async-start | bytes 262144 | tf_op jit(solution)/shard_map/all_to_all | solution.py:163
where the time goes:
time: 156 us; the launch traced here: 155 us
  blocking collectives  93.2 us (60%)
  waiting for transfers between devices  22.7 us (15%)
  local copies, waits for them, and re-layouts  17.4 us (11%)
  matrix products  11 us (7%)
  starting transfers between devices  7.73 us (5%)
  other arithmetic  2.2 us (1%)
    all_gather x1, blocking collectives, shards(): bias_all = lax.all_gather(bias_local, 'res', axis=1, tiled=True)  43.9 us
    all_gather x1, blocking collectives, shards(): piece = lax.all_gather(latter_factor, 'res', axis=0, tiled=True)  39.3 us
    all_to_all x1, blocking collectives, shards(): lax.all_to_all(alignment_after_rows, 'res', split_axis=1, concat_axis=0,...  9.91 us
    all_to_all x1, waiting for transfers between devices, shards(): lax.all_to_all(left_f, 'res', split_axis=0, concat_axis=2, tiled=True)  8.14 us
    all_to_all x1, waiting for transfers between devices, shards(): lax.all_to_all(right_f, 'res', split_axis=0, concat_axis=2, tiled=True)  7.35 us
    all_to_all x1, waiting for transfers between devices, shards(): lax.all_to_all(combined, 'res', split_axis=2, concat_axis=0, tiled=True)  7.17 us
    reshape x2, local copies, waits for them, and re-layouts, shards(): right_rows = piece.reshape(count, sequence_total, outer_chan)  3.78 us
    unnamed x26, local copies, waits for them, and re-layouts  3.38 us
  transfers between devices with their start and end apart: 3, of which 3 were waited for; matrix products, arithmetic and copies ran while one was open for 1% of the time, Pallas kernels for 0%

commit v1 on v0

--- a/solution.py
+++ b/solution.py
@@ -119,7 +119,9 @@
         .astype(jnp.bfloat16)
         .reshape(res_local, sequence_total * outer_chan)
     )
-    piece = lax.all_gather(latter_factor, "res", axis=0, tiled=True)
+    piece = jnp.concatenate(
+        lax.all_to_all(jnp.stack([latter_factor] * lax.axis_size("res")), "res", 0, 0), axis=0
+    )
     count = piece.shape[0]
     right_rows = piece.reshape(count, sequence_total, outer_chan)
     cross_product_result = (

time: 156 us -> 134 us (0.86)
  blocking collectives: 93.2 us -> 71.2 us
    all_gather x1 -> x0, blocking collectives: 39.3 us -> none  [shards(): piece = lax.all_gather(latter_factor, 'res', axis=0, tiled=True)]
    all_to_all x0 -> x1, blocking collectives: none -> 17.3 us  [shards(): lax.all_to_all(jnp.stack([latter_factor] * lax.axis_size('res')), 'res',...]
    another operation x0 -> x4, local copies, waits for them, and re-layouts: none -> 4.13 us  [the longest x2 3.78 us: shards(): right_rows = piece.reshape(count, sequence_total, outer_chan)]
    reshape x2 -> x0, local copies, waits for them, and re-layouts: 3.78 us -> none  [shards(): right_rows = piece.reshape(count, sequence_total, outer_chan)]
    unnamed x26 -> x25, local copies, waits for them, and re-layouts: 3.38 us -> 3.25 us
where the time goes in v1:
time: 134 us
  blocking collectives  71.2 us (53%)
  waiting for transfers between devices  22.7 us (17%)
  local copies, waits for them, and re-layouts  17.7 us (13%)
  matrix products  11 us (8%)
  starting transfers between devices  8.07 us (6%)
  other arithmetic  2.2 us (2%)
    all_gather x1, blocking collectives, shards(): bias_all = lax.all_gather(bias_local, 'res', axis=1, tiled=True)  43.9 us
    all_to_all x1, blocking collectives, shards(): lax.all_to_all(jnp.stack([latter_factor] * lax.axis_size('res')), 'res',...  17.3 us
    all_to_all x1, blocking collectives, shards(): lax.all_to_all(alignment_after_rows, 'res', split_axis=1, concat_axis=0,...  9.91 us
    all_to_all x1, waiting for transfers between devices, shards(): lax.all_to_all(left_f, 'res', split_axis=0, concat_axis=2, tiled=True)  8.14 us
    all_to_all x1, waiting for transfers between devices, shards(): lax.all_to_all(right_f, 'res', split_axis=0, concat_axis=2, tiled=True)  7.35 us
    all_to_all x1, waiting for transfers between devices, shards(): lax.all_to_all(combined, 'res', split_axis=2, concat_axis=0, tiled=True)  7.17 us
    another operation x2, local copies, waits for them, and re-layouts, shards(): right_rows = piece.reshape(count, sequence_total, outer_chan)  3.78 us
    unnamed x25, local copies, waits for them, and re-layouts  3.25 us
  transfers between devices with their start and end apart: 3, of which 3 were waited for; matrix products, arithmetic and copies ran while one was open for 1% of the time, Pallas kernels for 0%

profile of v1, /device:TPU:0, one launch (start us, length us, event | category | flops | bytes accessed | tf_op | source)
XLA Modules:
  0.0 133.9 jit_solution(4662460981922278406)
XLA Ops:
  0.7 0.7 add_multiply_fusion
  1.4 1.0 copy.74
  2.5 0.8 fusion.14
  3.4 43.9 %all_gather.3 = bf16[8,128,128]{2,0,1:T(8,128)(2,1)S(1)} all-gather(bf16[8,4,128]{2,0,1:T(8,128)(2,1)S(1)} %fusion.14), channel_id=1, replica_groups=mesh['crop'=1,'res'=32] {'res'}, dimensions={1}, use_global_device_ids=true | all-gather | bytes 270336 | tf_op jit(solution)/shard_map/all_gather | solution.py:94
  47.3 0.2 copy.76
  47.6 0.3 fusion.84
  47.9 0.2 multiply_reduce_fusion.3
  48.1 0.3 fusion.85
  48.5 0.7 fusion.83
  49.2 0.1 copy.73
  49.3 0.1 copy.72
  49.5 0.5 copy-done.1
  49.9 0.2 copy-done.2
  50.1 0.5 fusion.86
  50.6 1.3 convolution_add_fusion
  51.9 1.0 copy.71
  53.0 1.0 fusion.20
  54.0 1.1 copy.78
  55.2 1.1 fusion.11
  56.3 0.1 copy.79
  56.4 9.9 %all_to_all.53 = bf16[2,128,256]{2,0,1:T(2,128)(2,1)S(1)} all-to-all(bf16[2,128,256]{2,0,1:T(2,128)(2,1)S(1)} %copy.79), channel_id=1, replica_groups=mesh['crop'=1,'res'=32] {'res'}, dimensions={1} | all-to-all | bytes 262144 | tf_op jit(solution)/shard_map/all_to_all | solution.py:100
  66.4 0.2 reshape.161
  66.6 0.1 bitcast_reduce_fusion.1
  66.7 0.2 multiply_reduce_fusion.2
  66.9 0.3 fusion.87
  67.3 0.7 fusion.82
  68.0 0.2 copy.83
  68.2 0.2 copy.82
  68.4 0.5 fusion.88
  68.9 0.3 fusion.90
  69.2 1.1 copy.81
  70.3 1.2 fusion.19
  71.4 1.2 copy.85
  72.7 1.1 fusion.46
  73.8 0.1 fusion.81
  73.9 0.2 multiply_reduce_fusion.1
  74.1 0.3 convolution_convert_fusion.1
  74.4 0.1 copy.86
  74.5 0.1 stack_reshape.2
  74.7 0.2 stack.3
  74.9 17.3 %all_to_all.54 = bf16[32,4,2048]{2,1,0:T(4,128)(2,1)S(1)} all-to-all(bf16[32,4,2048]{2,1,0:T(4,128)(2,1)S(1)} %stack.3), channel_id=1, replica_groups=mesh['crop'=1,'res'=32] {'res'}, dimensions={0} | all-to-all | bytes 1048576 | tf_op jit(solution)/shard_map/all_to_all | solution.py:123
  92.2 1.2 reshape_reshape.3
  93.4 2.6 %copy.109 = bf16[128,64,32,1]{0,1,3,2:T(8,128)(2,1)S(1)} copy(bf16[128,64,32,1]{2,1,0,3:T(8,128)(2,1)S(1)} %bitcast.133) | data formatting | bytes 1048576 | tf_op jit(solution)/shard_map/reshape;reshape | solution.py:126
  96.0 0.4 fusion.6
  96.5 0.7 copy.88
  97.2 0.4 fusion.89
  97.6 0.3 convolution_bitcast_fusion
  98.0 0.1 fusion.25
  98.1 0.1 copy.97
  98.2 0.7 copy.98
  99.0 2.9 %all-to-all-start.3 = ((bf16[32,4,4,128]{3,1,2,0:T(4,128)(2,1)}), bf16[32,4,4,128]{3,1,2,0:T(4,128)(2,1)S(1)}, u32[]{:S(2)}, u32[]{:S(2)}) async-start(bf16[32,4,4,128]{3,1,2,0:T(4,128)(2,1)} %copy.98), calls=%async_computation.3 | async-start | bytes 262144 | tf_op jit(solution)/shard_map/all_to_all | solution.py:162
  101.9 0.1 copy.94
  102.0 0.7 copy.95
  102.7 7.4 %all-to-all-done.3 = bf16[32,4,4,128]{3,1,2,0:T(4,128)(2,1)S(1)} async-done(((bf16[32,4,4,128]{3,1,2,0:T(4,128)(2,1)}), bf16[32,4,4,128]{3,1,2,0:T(4,128)(2,1)S(1)}, u32[]{:S(2)}, u32[]{:S(2)}) %all-to-all-start.3) | async-done | bytes 131104 | tf_op jit(solution)/shard_map/all_to_all | solution.py:162
  110.1 2.6 %all-to-all-start.2 = ((bf16[32,4,4,128]{3,1,2,0:T(4,128)(2,1)}), bf16[32,4,4,128]{3,1,2,0:T(4,128)(2,1)S(1)}, u32[]{:S(2)}, u32[]{:S(2)}) async-start(bf16[32,4,4,128]{3,1,2,0:T(4,128)(2,1)} %copy.95), calls=%async_computation.2 | async-start | bytes 262144 | tf_op jit(solution)/shard_map/all_to_all | solution.py:161
  112.7 8.1 %all-to-all-done.2 = bf16[32,4,4,128]{3,1,2,0:T(4,128)(2,1)S(1)} async-done(((bf16[32,4,4,128]{3,1,2,0:T(4,128)(2,1)}), bf16[32,4,4,128]{3,1,2,0:T(4,128)(2,1)S(1)}, u32[]{:S(2)}, u32[]{:S(2)}) %all-to-all-start.2) | async-done | bytes 131104 | tf_op jit(solution)/shard_map/all_to_all | solution.py:161
  120.9 0.2 fusion.13
  121.1 0.8 copy.100
  121.9 2.6 %all-to-all-start.4 = ((bf16[1,4,128,128]{3,1,0,2:T(4,128)(2,1)}), bf16[1,4,128,128]{3,1,0,2:T(4,128)(2,1)S(1)}, u32[]{:S(2)}, u32[]{:S(2)}) async-start(bf16[1,4,128,128]{3,1,0,2:T(4,128)(2,1)} %copy.100), calls=%async_computation.4 | async-start | bytes 262144 | tf_op jit(solution)/shard_map/all_to_all | solution.py:165
  124.5 0.8 copy.104
  125.2 0.3 fusion.10
  125.5 7.2 %all-to-all-done.4 = bf16[1,4,128,128]{3,1,0,2:T(4,128)(2,1)S(1)} async-done(((bf16[1,4,128,128]{3,1,0,2:T(4,128)(2,1)}), bf16[1,4,128,128]{3,1,0,2:T(4,128)(2,1)S(1)}, u32[]{:S(2)}, u32[]{:S(2)}) %all-to-all-start.4) | async-done | bytes 131104 | tf_op jit(solution)/shard_map/all_to_all | solution.py:165
  132.9 0.2 fusion.12
  133.2 0.8 copy.105
  (45 shorter events, 0.7 us)
Async XLA Ops:
  0.6 47.5 %copy-start = (bf16[256,1024]{1,0:T(8,128)(2,1)S(1)}, bf16[256,1024]{1,0:T(8,128)(2,1)}, u32[]{:S(2)}) copy-start(bf16[256,1024]{1,0:T(8,128)(2,1)} %param.20) | copy-start | bytes 1572868
  0.6 46.9 %copy-start.9 = (bf16[23,256]{1,0:T(8,128)(2,1)S(1)}, bf16[23,256]{1,0:T(8,128)(2,1)}, u32[]{:S(2)}) copy-start(bf16[23,256]{1,0:T(8,128)(2,1)} %param.18) | copy-start | bytes 35332
  0.7 46.9 %copy-start.5 = (bf16[2,128,256]{2,1,0:T(8,128)(2,1)S(1)}, bf16[2,128,256]{2,1,0:T(8,128)(2,1)}, u32[]{:S(2)}) copy-start(bf16[2,128,256]{2,1,0:T(8,128)(2,1)} %param.16) | copy-start | bytes 393220
  0.7 46.9 %copy-start.10 = (s32[2,128]{1,0:T(2,128)S(1)}, s32[2,128]{1,0:T(2,128)}, u32[]{:S(2)}) copy-start(s32[2,128]{1,0:T(2,128)} %param.14) | copy-start | bytes 3076
  49.3 0.6 copy-start.1
  49.5 0.7 copy-start.2
  54.0 12.9 %copy-start.3 = (bf16[256,1024]{1,0:T(8,128)(2,1)S(1)}, bf16[256,1024]{1,0:T(8,128)(2,1)}, u32[]{:S(2)}) copy-start(bf16[256,1024]{1,0:T(8,128)(2,1)} %param.22) | copy-start | bytes 1572868
  71.4 2.7 %copy-start.7 = (bf16[256,64]{0,1:T(8,128)(2,1)S(1)}, bf16[256,64]{0,1:T(8,128)(2,1)}, u32[]{:S(2)}) copy-start(bf16[256,64]{0,1:T(8,128)(2,1)} %param.24) | copy-start | bytes 98308
  96.0 1.1 copy-start.4
  96.5 1.1 copy-start.6
  99.0 11.1 %all-to-all-start.3 = ((bf16[32,4,4,128]{3,1,2,0:T(4,128)(2,1)}), bf16[32,4,4,128]{3,1,2,0:T(4,128)(2,1)S(1)}, u32[]{:S(2)}, u32[]{:S(2)}) async-start(bf16[32,4,4,128]{3,1,2,0:T(4,128)(2,1)} %copy.98), calls=%async_computation.3 | async-start | bytes 262144 | tf_op jit(solution)/shard_map/all_to_all | solution.py:162
  102.0 30.9 %copy-start.8 = (bf16[128,128]{1,0:T(8,128)(2,1)S(1)}, bf16[128,128]{1,0:T(8,128)(2,1)}, u32[]{:S(2)}) copy-start(bf16[128,128]{1,0:T(8,128)(2,1)} %param.27) | copy-start | bytes 98308
  110.1 10.8 %all-to-all-start.2 = ((bf16[32,4,4,128]{3,1,2,0:T(4,128)(2,1)}), bf16[32,4,4,128]{3,1,2,0:T(4,128)(2,1)S(1)}, u32[]{:S(2)}, u32[]{:S(2)}) async-start(bf16[32,4,4,128]{3,1,2,0:T(4,128)(2,1)} %copy.95), calls=%async_computation.2 | async-start | bytes 262144 | tf_op jit(solution)/shard_map/all_to_all | solution.py:161
  121.9 10.8 %all-to-all-start.4 = ((bf16[1,4,128,128]{3,1,0,2:T(4,128)(2,1)}), bf16[1,4,128,128]{3,1,0,2:T(4,128)(2,1)S(1)}, u32[]{:S(2)}, u32[]{:S(2)}) async-start(bf16[1,4,128,128]{3,1,0,2:T(4,128)(2,1)} %copy.100), calls=%async_computation.4 | async-start | bytes 262144 | tf_op jit(solution)/shard_map/all_to_all | solution.py:165
